TPU v7x, 256 devices: a whole 4x4x8 slice. The times are simulated.
256 devices in a mesh: gx: 32 (over y, z_lo, core), gy: 8 (over z_hi, x).
Axes of the slice: x: 4, y: 4, z: 8 (z_hi: 2, z_lo: 4; z = z_hi * 4 + z_lo), core: 2. Of those that a mesh axis runs over, the one named last changes fastest.
Arguments:
- features: bfloat16 [32, 8, 3, 512, 192], P('gx', 'gy'), may hold values from -6 to 6
- weight: bfloat16 [5184, 192], replicated, may hold values from -0.078125 to 0.078125
- cotangent: bfloat16 [32, 8, 3, 64, 192], P('gx', 'gy'), may hold values from -6 to 6
- valid: int32 [32, 8, 3], P('gx', 'gy'), may hold values from 0 to 1, as said below
- local_rules: int32 [32, 8, 2, 12], P('gx', 'gy'), may hold values from 0 to 3, as said below
- local_codes: int32 [32, 8, 12], P('gx', 'gy'), may hold values from 0 to 7
- remote_rules: int32 [32, 8, 2, 3, 3], P('gx', 'gy'), may hold values from 0 to 3, as said below
- remote_codes: int32 [32, 8, 3, 3], P('gx', 'gy'), may hold values from 1 to 7, as said below
Outputs:
- output: bfloat16 [32, 8, 3, 64, 192], P('gx', 'gy')
- features_grad: bfloat16 [32, 8, 3, 512, 192], P('gx', 'gy')
- weight_grad: float32 [5184, 192], P('gx')
Inputs may be any that keep to these rules, and one draw needn't show every extreme that they name: `valid`: 1 marks a live brick slot; on each device the live slots come first and at least one slot is live. `local_rules`: entry [., ., 0, e] is a source slot and [., ., 1, e] a target slot of the same device; a target 3 marks an empty entry; non-empty entries name live slots. `remote_rules`: class m (third dimension) entry: a source slot on this device and a target slot on the device one step higher along gx (m = 0), along gy (m = 1) or along both (m = 2); a target 3 marks an empty entry; non-empty entries name live slots; devices at the upper end of an axis have no non-empty entries in the classes that cross it. `remote_codes`: the offset k mod 2 is 1 in classes 0 and 2, and the offset (k // 2) mod 2 is 1 in classes 1 and 2.
All inputs are finite; a program needn't handle non-finite values.
Results may differ from a plain program's by a relative error of at most 0.0045.
Values may be sent and summed in bfloat16 or wider, within the bound.
No kernel may reach another device: no remote copies, remote signals or barrier semaphores. Data moves between devices by JAX's collectives and lax.ppermute only.
A program may use at most 128 MiB of HBM per device.

v0:
```python
from functools import partial
import jax
import jax.numpy as jnp
import numpy as np
from jax import lax
from jax.sharding import PartitionSpec as P


def shifted(block, axis, distance):
    devices = range(lax.axis_size(axis))
    route = [(i - distance, i) for i in devices if i - distance in devices]
    return lax.ppermute(block, axis, route)


def offset_table(row_x, row_y, row_z):
    code_list = np.arange(8)[:, None]
    step_x = code_list % 2
    step_y = code_list // 2 % 2
    step_z = code_list // 4
    inside = (
        ((step_x == 0) | (row_x[None, :] == 0))
        & ((step_y == 0) | (row_y[None, :] == 0))
        & ((step_z == 0) | (row_z[None, :] == 0))
    )
    source_row = (
        (row_x[None, :] + 4 * step_x) * 25
        + (row_y[None, :] + 4 * step_y) * 5
        + row_z[None, :]
        + 4 * step_z
    )
    return np.where(inside, source_row, 125).astype(np.int32)


def full_table():
    voxel_ids = np.arange(64)
    return offset_table(voxel_ids // 16, voxel_ids // 4 % 4, voxel_ids % 4)


def face_x_table():
    face_ids = np.arange(16)
    return offset_table(np.zeros(16, np.int64), face_ids // 4, face_ids % 4)


def face_y_table():
    face_ids = np.arange(16)
    return offset_table(face_ids // 4, np.zeros(16, np.int64), face_ids % 4)


def corner_table():
    edge_ids = np.arange(4)
    return offset_table(np.zeros(4, np.int64), np.zeros(4, np.int64), edge_ids)


def brick_patches(one_brick):
    channels = one_brick.shape[-1]
    cube = one_brick.reshape(8, 8, 8, channels)
    padded = jnp.pad(cube, ((1, 2), (1, 2), (1, 2), (0, 0)))
    tap_list = []
    for along_x in range(3):
        for along_y in range(3):
            for along_z in range(3):
                tap_list.append(
                    padded[
                        along_x : along_x + 9 : 2,
                        along_y : along_y + 9 : 2,
                        along_z : along_z + 9 : 2,
                        :,
                    ]
                )
    return jnp.stack(tap_list, axis=3).reshape(125, 27 * channels)


def fold_front(values):
    even_part = values[0:4, 1]
    odd_part = values[1:5, 0] + values[0:4, 2]
    stacked = jnp.stack([even_part, odd_part], axis=1)
    return stacked.reshape((8,) + stacked.shape[2:])


def brick_fold(patch_grads, channels):
    tap_grads = patch_grads.reshape(5, 5, 5, 3, 3, 3, channels)
    ordered = jnp.transpose(tap_grads, (0, 3, 1, 4, 2, 5, 6))
    along_x = fold_front(ordered)
    along_x = jnp.transpose(along_x, (1, 2, 0, 3, 4, 5))
    along_y = fold_front(along_x)
    along_y = jnp.transpose(along_y, (2, 3, 1, 0, 4))
    along_z = fold_front(along_y)
    return jnp.transpose(along_z, (1, 2, 0, 3)).reshape(512, channels)


def row_positions(sources, code_list, row_table):
    return sources[:, None] * 126 + jnp.asarray(row_table)[code_list]


def pick_float(index, table):
    flat_index = index.reshape(-1)
    hits = (flat_index[:, None] == jnp.arange(table.shape[0], dtype=jnp.int32)[None, :]).astype(
        jnp.float32
    )
    picked = jnp.dot(
        hits, table, precision=lax.Precision.HIGHEST, preferred_element_type=jnp.float32
    )
    return picked.reshape(index.shape + (table.shape[1],))


def pick_half(index, table):
    hits = (index[:, None] == jnp.arange(table.shape[0], dtype=jnp.int32)[None, :]).astype(
        jnp.bfloat16
    )
    flat_table = table.reshape(table.shape[0], -1)
    picked = jnp.dot(hits, flat_table, preferred_element_type=jnp.float32).astype(jnp.bfloat16)
    return picked.reshape((index.shape[0],) + table.shape[1:])


def collect(targets, pieces, bricks):
    hits = (targets[None, :] == jnp.arange(bricks, dtype=jnp.int32)[:, None]).astype(jnp.float32)
    flat_pieces = pieces.reshape(pieces.shape[0], -1)
    return jnp.dot(
        hits, flat_pieces, precision=lax.Precision.HIGHEST, preferred_element_type=jnp.float32
    )


def shards(
    features, weight, cotangent, valid, local_rules, local_codes, remote_rules, remote_codes
):
    bricks = features.shape[2]
    channels = features.shape[-1]
    live_slots = valid[0, 0]
    live_float = live_slots.astype(jnp.float32)[:, None, None]
    masked = features[0, 0] * live_slots.astype(jnp.bfloat16)[:, None, None]
    flat_patches = jax.vmap(brick_patches)(masked).reshape(bricks * 125, 27 * channels)
    partials = jnp.dot(flat_patches, weight, preferred_element_type=jnp.float32).reshape(
        bricks, 125, channels
    )
    zero_rows = jnp.zeros((bricks, 1, channels), jnp.float32)
    partial_rows = jnp.concatenate([partials, zero_rows], axis=1).reshape(bricks * 126, channels)
    index_x = row_positions(remote_rules[0, 0, 0, 0], remote_codes[0, 0, 0], face_x_table())
    index_y = row_positions(remote_rules[0, 0, 0, 1], remote_codes[0, 0, 1], face_y_table())
    index_xy = row_positions(remote_rules[0, 0, 0, 2], remote_codes[0, 0, 2], corner_table())
    index_local = row_positions(local_rules[0, 0, 0], local_codes[0, 0], full_table())
    target_x = remote_rules[0, 0, 1, 0]
    target_y = remote_rules[0, 0, 1, 1]
    target_xy = remote_rules[0, 0, 1, 2]
    target_local = local_rules[0, 0, 1]
    pieces_x = pick_float(index_x, partial_rows)
    pieces_y = pick_float(index_y, partial_rows)
    pieces_xy = pick_float(index_xy, partial_rows)
    got_x, got_x_target = (
        shifted(pieces_x.astype(jnp.bfloat16), "gx", 1).astype(pieces_x.dtype),
        shifted(target_x, "gx", 1),
    )
    got_y, got_y_target = (
        shifted(pieces_y.astype(jnp.bfloat16), "gy", 1).astype(pieces_y.dtype),
        shifted(target_y, "gy", 1),
    )
    middle_xy, middle_target = shifted((pieces_xy, target_xy), "gx", 1)
    got_xy, got_xy_target = shifted((middle_xy, middle_target), "gy", 1)
    local_pieces = pick_float(index_local, partial_rows)
    totals = collect(target_local, local_pieces, bricks).reshape(bricks, 4, 4, 4, channels)
    face_x_sum = collect(got_x_target, got_x, bricks).reshape(bricks, 1, 4, 4, channels)
    face_y_sum = collect(got_y_target, got_y, bricks).reshape(bricks, 4, 1, 4, channels)
    edge_sum = collect(got_xy_target, got_xy, bricks).reshape(bricks, 1, 1, 4, channels)
    totals = totals + jnp.pad(face_x_sum, ((0, 0), (0, 3), (0, 0), (0, 0), (0, 0)))
    totals = totals + jnp.pad(face_y_sum, ((0, 0), (0, 0), (0, 3), (0, 0), (0, 0)))
    totals = totals + jnp.pad(edge_sum, ((0, 0), (0, 3), (0, 3), (0, 0), (0, 0)))
    output = (totals.reshape(bricks, 64, channels) * live_float).astype(jnp.bfloat16)
    grad_out = cotangent[0, 0] * live_slots.astype(jnp.bfloat16)[:, None, None]
    grad_pad = jnp.concatenate([grad_out, jnp.zeros((1, 64, channels), jnp.bfloat16)], axis=0)
    grad_cube = grad_pad.reshape(bricks + 1, 4, 4, 4, channels)
    back_x = pick_half(got_x_target, grad_cube[:, 0].reshape(bricks + 1, 16, channels))
    back_y = pick_half(got_y_target, grad_cube[:, :, 0].reshape(bricks + 1, 16, channels))
    back_xy = pick_half(got_xy_target, grad_cube[:, 0, 0])
    return_x = shifted(back_x, "gx", -1)
    return_y = shifted(back_y, "gy", -1)
    middle_back = shifted(back_xy, "gy", -1)
    return_xy = shifted(middle_back, "gx", -1)
    index_all = jnp.concatenate(
        [index_local.reshape(-1), index_x.reshape(-1), index_y.reshape(-1), index_xy.reshape(-1)]
    )
    value_all = jnp.concatenate(
        [
            pick_half(target_local, grad_pad).reshape(-1, channels),
            return_x.reshape(-1, channels),
            return_y.reshape(-1, channels),
            return_xy.reshape(-1, channels),
        ],
        axis=0,
    )
    row_hits = (jnp.arange(bricks * 126, dtype=jnp.int32)[:, None] == index_all[None, :]).astype(
        jnp.bfloat16
    )
    grad_rows = jnp.dot(row_hits, value_all, preferred_element_type=jnp.float32)
    grad_rounded = grad_rows.reshape(bricks, 126, channels)[:, :125].astype(jnp.bfloat16)
    flat_grads = grad_rounded.reshape(bricks * 125, channels)
    patch_grads = lax.dot_general(
        flat_grads, weight, (((1,), (1,)), ((), ())), preferred_element_type=jnp.float32
    )
    weight_local = lax.dot_general(
        flat_patches, flat_grads, (((0,), (0,)), ((), ())), preferred_element_type=jnp.float32
    )
    folded = jax.vmap(partial(brick_fold, channels=channels))(
        patch_grads.reshape(bricks, 125, 27 * channels)
    )
    features_grad = (folded * live_float).astype(jnp.bfloat16)
    summed = lax.psum(weight_local, ("gx", "gy"))
    share_rows = summed.shape[0] // lax.axis_size("gx")
    weight_share = lax.dynamic_slice_in_dim(
        summed, lax.axis_index("gx") * share_rows, share_rows, 0
    )
    return (output[None, None], features_grad[None, None], weight_share)


def solution(mesh):
    return jax.shard_map(
        shards,
        mesh=mesh,
        in_specs=(
            P("gx", "gy", None, None, None),
            P(),
            P("gx", "gy", None, None, None),
            P("gx", "gy", None),
            P("gx", "gy", None, None),
            P("gx", "gy", None),
            P("gx", "gy", None, None, None),
            P("gx", "gy", None, None),
        ),
        out_specs=(P("gx", "gy", None, None, None), P("gx", "gy", None, None, None), P("gx", None)),
        check_vma=False,
    )
```

profile of v0, /device:TPU:97, one launch (start us, length us, event | category | flops | bytes accessed | tf_op | source)
XLA Modules:
  0.0 1029.5 jit_solution(4450963363016071230)
XLA Ops:
  7.2 1.4 slice_bitcast_fusion.2
  8.6 2.4 collective-permute-start
  11.0 3.6 collective-permute-start.2
  14.6 2.2 collective-permute-start.4
  16.8 1.3 convert_bitcast_fusion
  18.1 1.3 copy.44
  20.2 23.2 %slice.156 = bf16[3,5,5,5,192]{4,3,2,1,0:T(8,128)(2,1)} slice(bf16[3,11,11,11,192]{4,3,2,1,0:T(8,128)(2,1)S(1)} %pad.18), slice={[0:3:1], [0:9:2], [0:9:2], [0:9:2], [0:192:1]} | slice | bytes 288000 | tf_op jit(solution)/shard_map/vmap()/slice | solution.py:63
  43.4 23.0 %slice.157 = bf16[3,5,5,5,192]{4,3,2,1,0:T(8,128)(2,1)} slice(bf16[3,11,11,11,192]{4,3,2,1,0:T(8,128)(2,1)S(1)} %pad.18), slice={[0:3:1], [0:9:2], [0:9:2], [1:10:2], [0:192:1]} | slice | bytes 288000 | tf_op jit(solution)/shard_map/vmap()/slice | solution.py:63
  66.4 23.1 %slice.158 = bf16[3,5,5,5,192]{4,3,2,1,0:T(8,128)(2,1)} slice(bf16[3,11,11,11,192]{4,3,2,1,0:T(8,128)(2,1)S(1)} %pad.18), slice={[0:3:1], [0:9:2], [0:9:2], [2:11:2], [0:192:1]} | slice | bytes 288000 | tf_op jit(solution)/shard_map/vmap()/slice | solution.py:63
  89.5 23.0 %slice.159 = bf16[3,5,5,5,192]{4,3,2,1,0:T(8,128)(2,1)} slice(bf16[3,11,11,11,192]{4,3,2,1,0:T(8,128)(2,1)S(1)} %pad.18), slice={[0:3:1], [0:9:2], [1:10:2], [0:9:2], [0:192:1]} | slice | bytes 288000 | tf_op jit(solution)/shard_map/vmap()/slice | solution.py:63
  112.5 23.0 %slice.160 = bf16[3,5,5,5,192]{4,3,2,1,0:T(8,128)(2,1)} slice(bf16[3,11,11,11,192]{4,3,2,1,0:T(8,128)(2,1)S(1)} %pad.18), slice={[0:3:1], [0:9:2], [1:10:2], [1:10:2], [0:192:1]} | slice | bytes 288000 | tf_op jit(solution)/shard_map/vmap()/slice | solution.py:63
  135.5 23.0 %slice.161 = bf16[3,5,5,5,192]{4,3,2,1,0:T(8,128)(2,1)} slice(bf16[3,11,11,11,192]{4,3,2,1,0:T(8,128)(2,1)S(1)} %pad.18), slice={[0:3:1], [0:9:2], [1:10:2], [2:11:2], [0:192:1]} | slice | bytes 288000 | tf_op jit(solution)/shard_map/vmap()/slice | solution.py:63
  158.5 23.0 %slice.162 = bf16[3,5,5,5,192]{4,3,2,1,0:T(8,128)(2,1)} slice(bf16[3,11,11,11,192]{4,3,2,1,0:T(8,128)(2,1)S(1)} %pad.18), slice={[0:3:1], [0:9:2], [2:11:2], [0:9:2], [0:192:1]} | slice | bytes 288000 | tf_op jit(solution)/shard_map/vmap()/slice | solution.py:63
  181.5 23.0 %slice.163 = bf16[3,5,5,5,192]{4,3,2,1,0:T(8,128)(2,1)} slice(bf16[3,11,11,11,192]{4,3,2,1,0:T(8,128)(2,1)S(1)} %pad.18), slice={[0:3:1], [0:9:2], [2:11:2], [1:10:2], [0:192:1]} | slice | bytes 288000 | tf_op jit(solution)/shard_map/vmap()/slice | solution.py:63
  204.5 23.0 %slice.164 = bf16[3,5,5,5,192]{4,3,2,1,0:T(8,128)(2,1)} slice(bf16[3,11,11,11,192]{4,3,2,1,0:T(8,128)(2,1)S(1)} %pad.18), slice={[0:3:1], [0:9:2], [2:11:2], [2:11:2], [0:192:1]} | slice | bytes 288000 | tf_op jit(solution)/shard_map/vmap()/slice | solution.py:63
  227.5 23.0 %slice.165 = bf16[3,5,5,5,192]{4,3,2,1,0:T(8,128)(2,1)} slice(bf16[3,11,11,11,192]{4,3,2,1,0:T(8,128)(2,1)S(1)} %pad.18), slice={[0:3:1], [1:10:2], [0:9:2], [0:9:2], [0:192:1]} | slice | bytes 288000 | tf_op jit(solution)/shard_map/vmap()/slice | solution.py:63
  250.5 23.0 %slice.166 = bf16[3,5,5,5,192]{4,3,2,1,0:T(8,128)(2,1)} slice(bf16[3,11,11,11,192]{4,3,2,1,0:T(8,128)(2,1)S(1)} %pad.18), slice={[0:3:1], [1:10:2], [0:9:2], [1:10:2], [0:192:1]} | slice | bytes 288000 | tf_op jit(solution)/shard_map/vmap()/slice | solution.py:63
  273.5 23.0 %slice.167 = bf16[3,5,5,5,192]{4,3,2,1,0:T(8,128)(2,1)} slice(bf16[3,11,11,11,192]{4,3,2,1,0:T(8,128)(2,1)S(1)} %pad.18), slice={[0:3:1], [1:10:2], [0:9:2], [2:11:2], [0:192:1]} | slice | bytes 288000 | tf_op jit(solution)/shard_map/vmap()/slice | solution.py:63
  296.6 23.0 %slice.168 = bf16[3,5,5,5,192]{4,3,2,1,0:T(8,128)(2,1)} slice(bf16[3,11,11,11,192]{4,3,2,1,0:T(8,128)(2,1)S(1)} %pad.18), slice={[0:3:1], [1:10:2], [1:10:2], [0:9:2], [0:192:1]} | slice | bytes 288000 | tf_op jit(solution)/shard_map/vmap()/slice | solution.py:63
  319.6 23.0 %slice.169 = bf16[3,5,5,5,192]{4,3,2,1,0:T(8,128)(2,1)} slice(bf16[3,11,11,11,192]{4,3,2,1,0:T(8,128)(2,1)S(1)} %pad.18), slice={[0:3:1], [1:10:2], [1:10:2], [1:10:2], [0:192:1]} | slice | bytes 288000 | tf_op jit(solution)/shard_map/vmap()/slice | solution.py:63
  342.6 23.0 %slice.170 = bf16[3,5,5,5,192]{4,3,2,1,0:T(8,128)(2,1)} slice(bf16[3,11,11,11,192]{4,3,2,1,0:T(8,128)(2,1)S(1)} %pad.18), slice={[0:3:1], [1:10:2], [1:10:2], [2:11:2], [0:192:1]} | slice | bytes 288000 | tf_op jit(solution)/shard_map/vmap()/slice | solution.py:63
  365.6 23.0 %slice.171 = bf16[3,5,5,5,192]{4,3,2,1,0:T(8,128)(2,1)} slice(bf16[3,11,11,11,192]{4,3,2,1,0:T(8,128)(2,1)S(1)} %pad.18), slice={[0:3:1], [1:10:2], [2:11:2], [0:9:2], [0:192:1]} | slice | bytes 288000 | tf_op jit(solution)/shard_map/vmap()/slice | solution.py:63
  388.7 23.0 %slice.172 = bf16[3,5,5,5,192]{4,3,2,1,0:T(8,128)(2,1)} slice(bf16[3,11,11,11,192]{4,3,2,1,0:T(8,128)(2,1)S(1)} %pad.18), slice={[0:3:1], [1:10:2], [2:11:2], [1:10:2], [0:192:1]} | slice | bytes 288000 | tf_op jit(solution)/shard_map/vmap()/slice | solution.py:63
  411.7 23.0 %slice.173 = bf16[3,5,5,5,192]{4,3,2,1,0:T(8,128)(2,1)} slice(bf16[3,11,11,11,192]{4,3,2,1,0:T(8,128)(2,1)S(1)} %pad.18), slice={[0:3:1], [1:10:2], [2:11:2], [2:11:2], [0:192:1]} | slice | bytes 288000 | tf_op jit(solution)/shard_map/vmap()/slice | solution.py:63
  434.7 23.0 %slice.174 = bf16[3,5,5,5,192]{4,3,2,1,0:T(8,128)(2,1)} slice(bf16[3,11,11,11,192]{4,3,2,1,0:T(8,128)(2,1)S(1)} %pad.18), slice={[0:3:1], [2:11:2], [0:9:2], [0:9:2], [0:192:1]} | slice | bytes 288000 | tf_op jit(solution)/shard_map/vmap()/slice | solution.py:63
  457.7 23.0 %slice.175 = bf16[3,5,5,5,192]{4,3,2,1,0:T(8,128)(2,1)} slice(bf16[3,11,11,11,192]{4,3,2,1,0:T(8,128)(2,1)S(1)} %pad.18), slice={[0:3:1], [2:11:2], [0:9:2], [1:10:2], [0:192:1]} | slice | bytes 288000 | tf_op jit(solution)/shard_map/vmap()/slice | solution.py:63
  480.7 23.0 %slice.176 = bf16[3,5,5,5,192]{4,3,2,1,0:T(8,128)(2,1)} slice(bf16[3,11,11,11,192]{4,3,2,1,0:T(8,128)(2,1)S(1)} %pad.18), slice={[0:3:1], [2:11:2], [0:9:2], [2:11:2], [0:192:1]} | slice | bytes 288000 | tf_op jit(solution)/shard_map/vmap()/slice | solution.py:63
  503.7 23.0 %slice.177 = bf16[3,5,5,5,192]{4,3,2,1,0:T(8,128)(2,1)} slice(bf16[3,11,11,11,192]{4,3,2,1,0:T(8,128)(2,1)S(1)} %pad.18), slice={[0:3:1], [2:11:2], [1:10:2], [0:9:2], [0:192:1]} | slice | bytes 288000 | tf_op jit(solution)/shard_map/vmap()/slice | solution.py:63
  526.7 23.0 %slice.178 = bf16[3,5,5,5,192]{4,3,2,1,0:T(8,128)(2,1)} slice(bf16[3,11,11,11,192]{4,3,2,1,0:T(8,128)(2,1)S(1)} %pad.18), slice={[0:3:1], [2:11:2], [1:10:2], [1:10:2], [0:192:1]} | slice | bytes 288000 | tf_op jit(solution)/shard_map/vmap()/slice | solution.py:63
  549.7 23.0 %slice.179 = bf16[3,5,5,5,192]{4,3,2,1,0:T(8,128)(2,1)} slice(bf16[3,11,11,11,192]{4,3,2,1,0:T(8,128)(2,1)S(1)} %pad.18), slice={[0:3:1], [2:11:2], [1:10:2], [2:11:2], [0:192:1]} | slice | bytes 288000 | tf_op jit(solution)/shard_map/vmap()/slice | solution.py:63
  572.7 23.0 %slice.180 = bf16[3,5,5,5,192]{4,3,2,1,0:T(8,128)(2,1)} slice(bf16[3,11,11,11,192]{4,3,2,1,0:T(8,128)(2,1)S(1)} %pad.18), slice={[0:3:1], [2:11:2], [2:11:2], [0:9:2], [0:192:1]} | slice | bytes 288000 | tf_op jit(solution)/shard_map/vmap()/slice | solution.py:63
  595.8 23.0 %slice.181 = bf16[3,5,5,5,192]{4,3,2,1,0:T(8,128)(2,1)} slice(bf16[3,11,11,11,192]{4,3,2,1,0:T(8,128)(2,1)S(1)} %pad.18), slice={[0:3:1], [2:11:2], [2:11:2], [1:10:2], [0:192:1]} | slice | bytes 288000 | tf_op jit(solution)/shard_map/vmap()/slice | solution.py:63
  618.8 3.0 slice.182
  636.5 4.8 copy.45
  641.3 9.1 dot_general.70
  650.4 3.6 fusion
  655.5 3.2 collective-permute-start.3
  660.3 4.2 collective-permute-start.1
  666.8 3.9 copy.55
  670.6 9.9 reshape.440
  686.9 1.2 reshape_reshape.8
  688.1 1.8 fusion.3
  689.9 1.2 reshape_reshape.7
  691.2 1.8 dot_general.74
  693.7 2.2 collective-permute-start.5
  696.8 2.6 collective-permute-start.6
  699.7 1.3 collective-permute-start.10
  702.7 1.9 collective-permute-start.8
  704.6 4.3 collective-permute-done.10
  708.9 2.3 collective-permute-start.11
  711.2 5.5 collective-permute-start.7
  718.2 1.3 collective-permute-start.9
  725.4 1.4 fusion.18
  726.8 1.5 fusion.6
  729.0 6.1 fusion.56
  735.1 7.4 convolution_bitcast_fusion
  742.4 6.0 fusion.53
  748.4 4.7 pad_maximum_fusion
  753.1 8.8 copy.56
  761.9 7.8 reshape.436
  769.7 2.6 fusion.54
  772.5 1.3 copy.81
  776.3 244.7 %all-reduce.8.cloned.1.call-done = f32[5184,192]{1,0:T(8,128)} async-done(((f32[5184,192]{1,0:T(8,128)}), f32[5184,192]{1,0:T(8,128)}) %all-reduce.8.cloned.1.call-update) | async-done | bytes 3981328 | tf_op jit(solution)/shard_map/psum | solution.py:205
  1021.1 1.6 constant_dynamic-slice_fusion
  (153 shorter events, 40.9 us)
Async XLA Ops:
  7.2 1013.9 %all-reduce.8.cloned.1.call-start = ((), (), s32[]{:S(2)}) async-start(), calls=%async_computation | async-start | bytes 10616832 | tf_op jit(solution)/shard_map/psum | solution.py:205
  8.6 691.1 %collective-permute-start = (s32[3]{0:T(128)}, s32[3]{0:T(128)}, u32[]{:S(2)}, u32[]{:S(2)}) collective-permute-start(s32[3]{0:T(128)} %get-tuple-element.12), channel_id=1, source_target_pairs={{0,8},{8,16},{16,24},{24,32},{32,40},{40,48},{48,56},{56,64},{64,7... | collective-permute-start | bytes 44 | tf_op jit(solution)/shard_map/ppermute | solution.py:12
  11.0 691.7 %collective-permute-start.2 = (s32[3]{0:T(128)}, s32[3]{0:T(128)}, u32[]{:S(2)}, u32[]{:S(2)}) collective-permute-start(s32[3]{0:T(128)} %get-tuple-element.14), channel_id=1, source_target_pairs={{0,1},{1,2},{2,3},{3,4},{4,5},{5,6},{6,7},{8,9},{9,10},{10,11},{11... | collective-permute-start | bytes 44 | tf_op jit(solution)/shard_map/ppermute | solution.py:12
  14.6 679.1 %collective-permute-start.4 = (s32[3]{0:T(128)}, s32[3]{0:T(128)}, u32[]{:S(2)}, u32[]{:S(2)}) collective-permute-start(s32[3]{0:T(128)} %get-tuple-element.17), channel_id=1, source_target_pairs={{0,8},{8,16},{16,24},{24,32},{32,40},{40,48},{48,56},{56,64},{64,7... | collective-permute-start | bytes 44 | tf_op jit(solution)/shard_map/ppermute | solution.py:12
  20.2 601.6 %copy-start.20 = (s32[1,1,3,3]{3,1,2,0:T(1,128)S(1)}, s32[1,1,3,3]{3,1,2,0:T(1,128)}, u32[]{:S(2)}) copy-start(s32[1,1,3,3]{3,1,2,0:T(1,128)} %param.19) | copy-start | bytes 112
  621.8 14.2 %copy-start.12 = (bf16[3,5,5,5,192]{4,3,2,1,0:T(8,128)(2,1)S(1)}, bf16[3,5,5,5,192]{4,3,2,1,0:T(8,128)(2,1)}, u32[]{:S(2)}) copy-start(bf16[3,5,5,5,192]{4,3,2,1,0:T(8,128)(2,1)} %slice.170) | copy-start | bytes 432004
  621.9 14.2 %copy-start.11 = (bf16[3,5,5,5,192]{4,3,2,1,0:T(8,128)(2,1)S(1)}, bf16[3,5,5,5,192]{4,3,2,1,0:T(8,128)(2,1)}, u32[]{:S(2)}) copy-start(bf16[3,5,5,5,192]{4,3,2,1,0:T(8,128)(2,1)} %slice.171) | copy-start | bytes 432004
  621.9 14.2 %copy-start.10 = (bf16[3,5,5,5,192]{4,3,2,1,0:T(8,128)(2,1)S(1)}, bf16[3,5,5,5,192]{4,3,2,1,0:T(8,128)(2,1)}, u32[]{:S(2)}) copy-start(bf16[3,5,5,5,192]{4,3,2,1,0:T(8,128)(2,1)} %slice.172) | copy-start | bytes 432004
  621.9 14.3 %copy-start.9 = (bf16[3,5,5,5,192]{4,3,2,1,0:T(8,128)(2,1)S(1)}, bf16[3,5,5,5,192]{4,3,2,1,0:T(8,128)(2,1)}, u32[]{:S(2)}) copy-start(bf16[3,5,5,5,192]{4,3,2,1,0:T(8,128)(2,1)} %slice.173) | copy-start | bytes 432004
  621.9 14.3 %copy-start.8 = (bf16[3,5,5,5,192]{4,3,2,1,0:T(8,128)(2,1)S(1)}, bf16[3,5,5,5,192]{4,3,2,1,0:T(8,128)(2,1)}, u32[]{:S(2)}) copy-start(bf16[3,5,5,5,192]{4,3,2,1,0:T(8,128)(2,1)} %slice.174) | copy-start | bytes 432004
  621.9 14.3 %copy-start.7 = (bf16[3,5,5,5,192]{4,3,2,1,0:T(8,128)(2,1)S(1)}, bf16[3,5,5,5,192]{4,3,2,1,0:T(8,128)(2,1)}, u32[]{:S(2)}) copy-start(bf16[3,5,5,5,192]{4,3,2,1,0:T(8,128)(2,1)} %slice.175) | copy-start | bytes 432004
  621.9 14.3 %copy-start.6 = (bf16[3,5,5,5,192]{4,3,2,1,0:T(8,128)(2,1)S(1)}, bf16[3,5,5,5,192]{4,3,2,1,0:T(8,128)(2,1)}, u32[]{:S(2)}) copy-start(bf16[3,5,5,5,192]{4,3,2,1,0:T(8,128)(2,1)} %slice.176) | copy-start | bytes 432004
  621.9 14.4 %copy-start.5 = (bf16[3,5,5,5,192]{4,3,2,1,0:T(8,128)(2,1)S(1)}, bf16[3,5,5,5,192]{4,3,2,1,0:T(8,128)(2,1)}, u32[]{:S(2)}) copy-start(bf16[3,5,5,5,192]{4,3,2,1,0:T(8,128)(2,1)} %slice.177) | copy-start | bytes 432004
  621.9 14.4 %copy-start.4 = (bf16[3,5,5,5,192]{4,3,2,1,0:T(8,128)(2,1)S(1)}, bf16[3,5,5,5,192]{4,3,2,1,0:T(8,128)(2,1)}, u32[]{:S(2)}) copy-start(bf16[3,5,5,5,192]{4,3,2,1,0:T(8,128)(2,1)} %slice.178) | copy-start | bytes 432004
  621.9 14.4 %copy-start.3 = (bf16[3,5,5,5,192]{4,3,2,1,0:T(8,128)(2,1)S(1)}, bf16[3,5,5,5,192]{4,3,2,1,0:T(8,128)(2,1)}, u32[]{:S(2)}) copy-start(bf16[3,5,5,5,192]{4,3,2,1,0:T(8,128)(2,1)} %slice.179) | copy-start | bytes 432004
  621.9 14.5 %copy-start.2 = (bf16[3,5,5,5,192]{4,3,2,1,0:T(8,128)(2,1)S(1)}, bf16[3,5,5,5,192]{4,3,2,1,0:T(8,128)(2,1)}, u32[]{:S(2)}) copy-start(bf16[3,5,5,5,192]{4,3,2,1,0:T(8,128)(2,1)} %slice.180) | copy-start | bytes 432004
  622.0 14.5 %copy-start.1 = (bf16[3,5,5,5,192]{4,3,2,1,0:T(8,128)(2,1)S(1)}, bf16[3,5,5,5,192]{4,3,2,1,0:T(8,128)(2,1)}, u32[]{:S(2)}) copy-start(bf16[3,5,5,5,192]{4,3,2,1,0:T(8,128)(2,1)} %slice.181) | copy-start | bytes 432004
  641.3 9.1 copy-start
  641.3 13.2 %copy-start.18 = (s32[8,16]{1,0:T(8,128)S(1)}, s32[8,16]{1,0:T(8,128)}, u32[]{:S(2)}) copy-start(s32[8,16]{1,0:T(8,128)} %constant.35.clone) | copy-start | bytes 1540
  641.3 17.4 %copy-start.22 = (s32[1,1,12]{2,1,0:T(1,128)S(1)}, s32[1,1,12]{2,1,0:T(1,128)}, u32[]{:S(2)}) copy-start(s32[1,1,12]{2,1,0:T(1,128)} %param.17) | copy-start | bytes 148
  641.3 17.5 %copy-start.17 = (s32[8,16]{1,0:T(8,128)S(1)}, s32[8,16]{1,0:T(8,128)}, u32[]{:S(2)}) copy-start(s32[8,16]{1,0:T(8,128)} %constant.34.clone) | copy-start | bytes 1540
  641.3 24.5 %copy-start.15 = (bf16[1,1,3,64,192]{4,3,2,1,0:T(8,128)(2,1)S(1)}, bf16[1,1,3,64,192]{4,3,2,1,0:T(8,128)(2,1)}, u32[]{:S(2)}) copy-start(bf16[1,1,3,64,192]{4,3,2,1,0:T(8,128)(2,1)} %param.14) | copy-start | bytes 221188
  655.5 64.0 %collective-permute-start.3 = (bf16[3,16,192]{2,1,0:T(8,128)(2,1)S(1)}, bf16[3,16,192]{2,1,0:T(8,128)(2,1)}, u32[]{:S(2)}, u32[]{:S(2)}) collective-permute-start(bf16[3,16,192]{2,1,0:T(8,128)(2,1)S(1)} %convolution_convert_fusion.3), channel_id=1, source_target_pairs={{0,1},{1,2},{2,3},{3,4},{4,5},{5,6},{6,7},{8,9},{9,10},{10,11},{11... | collective-permute-start | bytes 55304 | tf_op jit(solution)/shard_map/ppermute | solution.py:12
  660.3 21.1 %copy-start.16 = (s32[8,4]{1,0:T(8,128)S(1)}, s32[8,4]{1,0:T(8,128)}, u32[]{:S(2)}) copy-start(s32[8,4]{1,0:T(8,128)} %constant.36.clone) | copy-start | bytes 388
  660.3 60.1 %collective-permute-start.1 = (bf16[3,16,192]{2,1,0:T(8,128)(2,1)}, bf16[3,16,192]{2,1,0:T(8,128)(2,1)}, u32[]{:S(2)}, u32[]{:S(2)}) collective-permute-start(bf16[3,16,192]{2,1,0:T(8,128)(2,1)} %convolution_convert_fusion.4), channel_id=1, source_target_pairs={{0,8},{8,16},{16,24},{24,32},{32,40},{40,48},{48,56},{56,64},{64,7... | collective-permute-start | bytes 55304 | tf_op jit(solution)/shard_map/ppermute | solution.py:12
  665.8 19.2 %copy-start.13 = (s32[8,64]{1,0:T(8,128)S(1)}, s32[8,64]{1,0:T(8,128)}, u32[]{:S(2)}) copy-start(s32[8,64]{1,0:T(8,128)} %constant.37.clone) | copy-start | bytes 6148
  665.9 0.7 copy-start.14
  666.7 19.0 %slice-start = ((bf16[4,4,4,4,192]{4,3,2,1,0:T(4,128)(2,1)}), bf16[4,1,4,4,192]{4,3,2,1,0:T(4,128)(2,1)S(1)}, s32[]{:S(2)}) async-start(bf16[4,4,4,4,192]{4,3,2,1,0:T(4,128)(2,1)} %copy-done.14), calls=%async_computation.1 | async-start | bytes 65536 | tf_op jit(solution)/shard_map/slice | solution.py:170
  666.8 19.7 %slice-start.1 = ((bf16[4,4,4,4,192]{4,3,2,1,0:T(4,128)(2,1)}), bf16[4,4,1,4,192]{4,3,2,1,0:T(4,128)(2,1)S(1)}, s32[]{:S(2)}) async-start(bf16[4,4,4,4,192]{4,3,2,1,0:T(4,128)(2,1)} %copy-done.14), calls=%async_computation.2 | async-start | bytes 65536 | tf_op jit(solution)/shard_map/slice | solution.py:171
  693.7 3.1 collective-permute-start.5
  696.8 23.5 %copy-start.21 = (s32[3]{0:T(128)}, s32[3]{0:T(128)S(1)}, u32[]{:S(2)}) copy-start(s32[3]{0:T(128)S(1)} %collective-permute-done.5) | copy-start | bytes 40
  696.8 14.4 %collective-permute-start.6 = (f32[3,4,192]{2,1,0:T(4,128)}, f32[3,4,192]{2,1,0:T(4,128)}, u32[]{:S(2)}, u32[]{:S(2)}) collective-permute-start(f32[3,4,192]{2,1,0:T(4,128)} %fusion.28), channel_id=1, source_target_pairs={{0,8},{8,16},{16,24},{24,32},{32,40},{40,48},{48,56},{56,64},{64,7... | collective-permute-start | bytes 27656 | tf_op jit(solution)/shard_map/ppermute | solution.py:12
  699.7 9.1 collective-permute-start.10
  702.7 24.2 %collective-permute-start.8 = (bf16[3,16,192]{2,1,0:T(8,128)(2,1)}, bf16[3,16,192]{2,1,0:T(8,128)(2,1)}, u32[]{:S(2)}, u32[]{:S(2)}) collective-permute-start(bf16[3,16,192]{2,1,0:T(8,128)(2,1)} %reshape.429), channel_id=1, source_target_pairs={{8,0},{16,8},{24,16},{32,24},{40,32},{48,40},{56,48},{64,56},{72,6... | collective-permute-start | bytes 55304 | tf_op jit(solution)/shard_map/ppermute | solution.py:12
  708.9 9.3 collective-permute-start.11
  711.2 10.2 collective-permute-start.7
  718.2 8.6 collective-permute-start.9
  772.5 2.5 copy-start.19
Sparse Core Ops, SparseCore 0:
  735.2 285.8 all-reduce.7
where the time goes:
time: 1030 us
  local copies, waits for them, and re-layouts  683 us (66%)
  waiting for transfers between devices  250 us (24%)
  starting transfers between devices  32.8 us (3%)
  matrix products  27.9 us (3%)
  other arithmetic  20.6 us (2%)
  between operations  14.9 us (1%)
    slice x27, local copies, waits for them, and re-layouts, brick_patches(): padded[along_x:along_x + 9:2, along_y:along_y + 9:2, along_z:along_z + 9:...  602 us
    psum x1, waiting for transfers between devices, shards(): summed = lax.psum(weight_local, ('gx', 'gy'))  245 us
    ppermute x12, starting transfers between devices, shifted(): return lax.ppermute(block, axis, route)  32.8 us
    unnamed x76, local copies, waits for them, and re-layouts  21.5 us
  transfers between devices with their start and end apart: 13, of which 3 were waited for; matrix products, arithmetic and copies ran while one was open for 70% of the time, Pallas kernels for 0%

commit v1 on v0

--- a/solution.py
+++ b/solution.py
@@ -202,7 +202,7 @@
         patch_grads.reshape(bricks, 125, 27 * channels)
     )
     features_grad = (folded * live_float).astype(jnp.bfloat16)
-    summed = lax.psum(weight_local, ("gx", "gy"))
+    summed = lax.psum(lax.psum(weight_local, "gx"), "gy")
     share_rows = summed.shape[0] // lax.axis_size("gx")
     weight_share = lax.dynamic_slice_in_dim(
         summed, lax.axis_index("gx") * share_rows, share_rows, 0

time: 1030 us -> 1260 us (1.22); the launches traced: 1030 us -> 1250 us
  waiting for transfers between devices: 250 us -> 446 us
  local copies, waits for them, and re-layouts: 683 us -> 701 us
    psum x1 -> x2, waiting for transfers between devices: 245 us -> 443 us  [shards(): summed = lax.psum(lax.psum(weight_local, 'gx'), 'gy')]
    unnamed x76 -> x84, local copies, waits for them, and re-layouts: 21.5 us -> 39.2 us
  transfers between devices with their start and end apart: 13 -> 14, of which waited for: 3 -> 4; matrix products, arithmetic and copies ran while one was open for 70% -> 59% of each run, Pallas kernels for 0% -> 0%
where the time goes in v1:
time: 1260 us; the launch traced here: 1250 us
  local copies, waits for them, and re-layouts  701 us (56%)
  waiting for transfers between devices  446 us (35%)
  starting transfers between devices  40.4 us (3%)
  matrix products  24.2 us (2%)
  other arithmetic  18.7 us (1%)
  between operations  14.8 us (1%)
    slice x27, local copies, waits for them, and re-layouts, brick_patches(): padded[along_x:along_x + 9:2, along_y:along_y + 9:2, along_z:along_z + 9:...  602 us
    psum x2, waiting for transfers between devices, shards(): summed = lax.psum(lax.psum(weight_local, 'gx'), 'gy')  443 us
    ppermute x12, starting transfers between devices, shifted(): return lax.ppermute(block, axis, route)  40.2 us
    unnamed x84, local copies, waits for them, and re-layouts  39.2 us
  transfers between devices with their start and end apart: 14, of which 4 were waited for; matrix products, arithmetic and copies ran while one was open for 59% of the time, Pallas kernels for 0%

profile of v1, /device:TPU:97, one launch (start us, length us, event | category | flops | bytes accessed | tf_op | source)
XLA Modules:
  0.0 1245.2 jit_solution(2619998340919093440)
XLA Ops:
  8.0 2.4 collective-permute-start
  10.4 3.1 collective-permute-start.2
  13.5 2.2 collective-permute-start.4
  20.4 23.2 %slice.156 = bf16[3,5,5,5,192]{4,3,2,1,0:T(8,128)(2,1)} slice(bf16[3,11,11,11,192]{4,3,2,1,0:T(8,128)(2,1)S(1)} %pad.18), slice={[0:3:1], [0:9:2], [0:9:2], [0:9:2], [0:192:1]} | slice | bytes 288000 | tf_op jit(solution)/shard_map/vmap()/slice | solution.py:63
  43.6 23.0 %slice.157 = bf16[3,5,5,5,192]{4,3,2,1,0:T(8,128)(2,1)} slice(bf16[3,11,11,11,192]{4,3,2,1,0:T(8,128)(2,1)S(1)} %pad.18), slice={[0:3:1], [0:9:2], [0:9:2], [1:10:2], [0:192:1]} | slice | bytes 288000 | tf_op jit(solution)/shard_map/vmap()/slice | solution.py:63
  66.6 23.0 %slice.158 = bf16[3,5,5,5,192]{4,3,2,1,0:T(8,128)(2,1)} slice(bf16[3,11,11,11,192]{4,3,2,1,0:T(8,128)(2,1)S(1)} %pad.18), slice={[0:3:1], [0:9:2], [0:9:2], [2:11:2], [0:192:1]} | slice | bytes 288000 | tf_op jit(solution)/shard_map/vmap()/slice | solution.py:63
  89.6 23.0 %slice.159 = bf16[3,5,5,5,192]{4,3,2,1,0:T(8,128)(2,1)} slice(bf16[3,11,11,11,192]{4,3,2,1,0:T(8,128)(2,1)S(1)} %pad.18), slice={[0:3:1], [0:9:2], [1:10:2], [0:9:2], [0:192:1]} | slice | bytes 288000 | tf_op jit(solution)/shard_map/vmap()/slice | solution.py:63
  112.7 23.0 %slice.160 = bf16[3,5,5,5,192]{4,3,2,1,0:T(8,128)(2,1)} slice(bf16[3,11,11,11,192]{4,3,2,1,0:T(8,128)(2,1)S(1)} %pad.18), slice={[0:3:1], [0:9:2], [1:10:2], [1:10:2], [0:192:1]} | slice | bytes 288000 | tf_op jit(solution)/shard_map/vmap()/slice | solution.py:63
  135.7 23.0 %slice.161 = bf16[3,5,5,5,192]{4,3,2,1,0:T(8,128)(2,1)} slice(bf16[3,11,11,11,192]{4,3,2,1,0:T(8,128)(2,1)S(1)} %pad.18), slice={[0:3:1], [0:9:2], [1:10:2], [2:11:2], [0:192:1]} | slice | bytes 288000 | tf_op jit(solution)/shard_map/vmap()/slice | solution.py:63
  158.7 23.0 %slice.162 = bf16[3,5,5,5,192]{4,3,2,1,0:T(8,128)(2,1)} slice(bf16[3,11,11,11,192]{4,3,2,1,0:T(8,128)(2,1)S(1)} %pad.18), slice={[0:3:1], [0:9:2], [2:11:2], [0:9:2], [0:192:1]} | slice | bytes 288000 | tf_op jit(solution)/shard_map/vmap()/slice | solution.py:63
  181.7 23.0 %slice.163 = bf16[3,5,5,5,192]{4,3,2,1,0:T(8,128)(2,1)} slice(bf16[3,11,11,11,192]{4,3,2,1,0:T(8,128)(2,1)S(1)} %pad.18), slice={[0:3:1], [0:9:2], [2:11:2], [1:10:2], [0:192:1]} | slice | bytes 288000 | tf_op jit(solution)/shard_map/vmap()/slice | solution.py:63
  204.8 23.0 %slice.164 = bf16[3,5,5,5,192]{4,3,2,1,0:T(8,128)(2,1)} slice(bf16[3,11,11,11,192]{4,3,2,1,0:T(8,128)(2,1)S(1)} %pad.18), slice={[0:3:1], [0:9:2], [2:11:2], [2:11:2], [0:192:1]} | slice | bytes 288000 | tf_op jit(solution)/shard_map/vmap()/slice | solution.py:63
  227.8 23.0 %slice.165 = bf16[3,5,5,5,192]{4,3,2,1,0:T(8,128)(2,1)} slice(bf16[3,11,11,11,192]{4,3,2,1,0:T(8,128)(2,1)S(1)} %pad.18), slice={[0:3:1], [1:10:2], [0:9:2], [0:9:2], [0:192:1]} | slice | bytes 288000 | tf_op jit(solution)/shard_map/vmap()/slice | solution.py:63
  250.8 23.1 %slice.166 = bf16[3,5,5,5,192]{4,3,2,1,0:T(8,128)(2,1)} slice(bf16[3,11,11,11,192]{4,3,2,1,0:T(8,128)(2,1)S(1)} %pad.18), slice={[0:3:1], [1:10:2], [0:9:2], [1:10:2], [0:192:1]} | slice | bytes 288000 | tf_op jit(solution)/shard_map/vmap()/slice | solution.py:63
  273.8 23.1 %slice.167 = bf16[3,5,5,5,192]{4,3,2,1,0:T(8,128)(2,1)} slice(bf16[3,11,11,11,192]{4,3,2,1,0:T(8,128)(2,1)S(1)} %pad.18), slice={[0:3:1], [1:10:2], [0:9:2], [2:11:2], [0:192:1]} | slice | bytes 288000 | tf_op jit(solution)/shard_map/vmap()/slice | solution.py:63
  296.9 23.0 %slice.168 = bf16[3,5,5,5,192]{4,3,2,1,0:T(8,128)(2,1)} slice(bf16[3,11,11,11,192]{4,3,2,1,0:T(8,128)(2,1)S(1)} %pad.18), slice={[0:3:1], [1:10:2], [1:10:2], [0:9:2], [0:192:1]} | slice | bytes 288000 | tf_op jit(solution)/shard_map/vmap()/slice | solution.py:63
  319.9 23.0 %slice.169 = bf16[3,5,5,5,192]{4,3,2,1,0:T(8,128)(2,1)} slice(bf16[3,11,11,11,192]{4,3,2,1,0:T(8,128)(2,1)S(1)} %pad.18), slice={[0:3:1], [1:10:2], [1:10:2], [1:10:2], [0:192:1]} | slice | bytes 288000 | tf_op jit(solution)/shard_map/vmap()/slice | solution.py:63
  342.9 23.0 %slice.170 = bf16[3,5,5,5,192]{4,3,2,1,0:T(8,128)(2,1)} slice(bf16[3,11,11,11,192]{4,3,2,1,0:T(8,128)(2,1)S(1)} %pad.18), slice={[0:3:1], [1:10:2], [1:10:2], [2:11:2], [0:192:1]} | slice | bytes 288000 | tf_op jit(solution)/shard_map/vmap()/slice | solution.py:63
  366.0 23.0 %slice.171 = bf16[3,5,5,5,192]{4,3,2,1,0:T(8,128)(2,1)} slice(bf16[3,11,11,11,192]{4,3,2,1,0:T(8,128)(2,1)S(1)} %pad.18), slice={[0:3:1], [1:10:2], [2:11:2], [0:9:2], [0:192:1]} | slice | bytes 288000 | tf_op jit(solution)/shard_map/vmap()/slice | solution.py:63
  389.0 23.1 %slice.172 = bf16[3,5,5,5,192]{4,3,2,1,0:T(8,128)(2,1)} slice(bf16[3,11,11,11,192]{4,3,2,1,0:T(8,128)(2,1)S(1)} %pad.18), slice={[0:3:1], [1:10:2], [2:11:2], [1:10:2], [0:192:1]} | slice | bytes 288000 | tf_op jit(solution)/shard_map/vmap()/slice | solution.py:63
  412.1 23.0 %slice.173 = bf16[3,5,5,5,192]{4,3,2,1,0:T(8,128)(2,1)} slice(bf16[3,11,11,11,192]{4,3,2,1,0:T(8,128)(2,1)S(1)} %pad.18), slice={[0:3:1], [1:10:2], [2:11:2], [2:11:2], [0:192:1]} | slice | bytes 288000 | tf_op jit(solution)/shard_map/vmap()/slice | solution.py:63
  435.1 23.0 %slice.174 = bf16[3,5,5,5,192]{4,3,2,1,0:T(8,128)(2,1)} slice(bf16[3,11,11,11,192]{4,3,2,1,0:T(8,128)(2,1)S(1)} %pad.18), slice={[0:3:1], [2:11:2], [0:9:2], [0:9:2], [0:192:1]} | slice | bytes 288000 | tf_op jit(solution)/shard_map/vmap()/slice | solution.py:63
  458.1 23.0 %slice.175 = bf16[3,5,5,5,192]{4,3,2,1,0:T(8,128)(2,1)} slice(bf16[3,11,11,11,192]{4,3,2,1,0:T(8,128)(2,1)S(1)} %pad.18), slice={[0:3:1], [2:11:2], [0:9:2], [1:10:2], [0:192:1]} | slice | bytes 288000 | tf_op jit(solution)/shard_map/vmap()/slice | solution.py:63
  481.1 23.0 %slice.176 = bf16[3,5,5,5,192]{4,3,2,1,0:T(8,128)(2,1)} slice(bf16[3,11,11,11,192]{4,3,2,1,0:T(8,128)(2,1)S(1)} %pad.18), slice={[0:3:1], [2:11:2], [0:9:2], [2:11:2], [0:192:1]} | slice | bytes 288000 | tf_op jit(solution)/shard_map/vmap()/slice | solution.py:63
  504.1 23.0 %slice.177 = bf16[3,5,5,5,192]{4,3,2,1,0:T(8,128)(2,1)} slice(bf16[3,11,11,11,192]{4,3,2,1,0:T(8,128)(2,1)S(1)} %pad.18), slice={[0:3:1], [2:11:2], [1:10:2], [0:9:2], [0:192:1]} | slice | bytes 288000 | tf_op jit(solution)/shard_map/vmap()/slice | solution.py:63
  527.1 23.0 %slice.178 = bf16[3,5,5,5,192]{4,3,2,1,0:T(8,128)(2,1)} slice(bf16[3,11,11,11,192]{4,3,2,1,0:T(8,128)(2,1)S(1)} %pad.18), slice={[0:3:1], [2:11:2], [1:10:2], [1:10:2], [0:192:1]} | slice | bytes 288000 | tf_op jit(solution)/shard_map/vmap()/slice | solution.py:63
  550.1 23.0 %slice.179 = bf16[3,5,5,5,192]{4,3,2,1,0:T(8,128)(2,1)} slice(bf16[3,11,11,11,192]{4,3,2,1,0:T(8,128)(2,1)S(1)} %pad.18), slice={[0:3:1], [2:11:2], [1:10:2], [2:11:2], [0:192:1]} | slice | bytes 288000 | tf_op jit(solution)/shard_map/vmap()/slice | solution.py:63
  573.2 23.0 %slice.180 = bf16[3,5,5,5,192]{4,3,2,1,0:T(8,128)(2,1)} slice(bf16[3,11,11,11,192]{4,3,2,1,0:T(8,128)(2,1)S(1)} %pad.18), slice={[0:3:1], [2:11:2], [2:11:2], [0:9:2], [0:192:1]} | slice | bytes 288000 | tf_op jit(solution)/shard_map/vmap()/slice | solution.py:63
  596.2 23.0 %slice.181 = bf16[3,5,5,5,192]{4,3,2,1,0:T(8,128)(2,1)} slice(bf16[3,11,11,11,192]{4,3,2,1,0:T(8,128)(2,1)S(1)} %pad.18), slice={[0:3:1], [2:11:2], [2:11:2], [1:10:2], [0:192:1]} | slice | bytes 288000 | tf_op jit(solution)/shard_map/vmap()/slice | solution.py:63
  619.2 3.0 slice.182
  625.6 1.8 bitcast_dynamic-update-slice_fusion.26
  627.8 1.7 bitcast_dynamic-update-slice_fusion.25
  629.5 1.7 bitcast_dynamic-update-slice_fusion.24
  631.2 1.7 bitcast_dynamic-update-slice_fusion.23
  632.9 1.7 bitcast_dynamic-update-slice_fusion.22
  634.6 1.7 bitcast_dynamic-update-slice_fusion.21
  636.3 1.7 bitcast_dynamic-update-slice_fusion.20
  638.0 1.7 bitcast_dynamic-update-slice_fusion.19
  639.7 1.7 bitcast_dynamic-update-slice_fusion.18
  641.4 1.7 bitcast_dynamic-update-slice_fusion.17
  643.1 1.7 bitcast_dynamic-update-slice_fusion.16
  646.6 1.7 bitcast_dynamic-update-slice_fusion.14
  659.1 2.1 collective-permute-start.8
  661.3 3.1 collective-permute-start.5
  670.0 5.6 collective-permute-start.11
  676.2 8.1 copy.45
  684.3 9.9 reshape.440
  695.6 6.1 fusion.56
  702.0 9.2 dot_general.70
  711.1 3.6 fusion
  715.6 6.0 collective-permute-start.3
  721.8 6.4 collective-permute-start.6
  728.6 2.1 collective-permute-start.1
  730.9 4.5 collective-permute-start.7
  736.2 3.9 copy.55
  741.4 1.8 dot_general.74
  746.6 247.8 %all-reduce.9.cloned.1.call-done = f32[5184,192]{1,0:T(8,128)} async-done(((f32[5184,192]{1,0:T(8,128)}), f32[5184,192]{1,0:T(8,128)}) %all-reduce.9.cloned.1.call-update) | async-done | bytes 3981328 | tf_op jit(solution)/shard_map/psum | solution.py:205
  1000.2 7.4 convolution_bitcast_fusion
  1007.6 6.0 fusion.53
  1013.6 4.7 pad_maximum_fusion
  1018.2 8.8 copy.56
  1027.1 7.8 reshape.436
  1034.8 2.5 fusion.54
  1041.4 195.4 %all-reduce.11.cloned.1.call-done = f32[5184,192]{1,0:T(8,128)} async-done(((f32[5184,192]{1,0:T(8,128)}), f32[5184,192]{1,0:T(8,128)}) %all-reduce.11.cloned.1.call-update) | async-done | bytes 3981328 | tf_op jit(solution)/shard_map/psum | solution.py:205
  (162 shorter events, 47.6 us)
Async XLA Ops:
  7.2 987.2 %all-reduce.9.cloned.1.call-start = ((), (), s32[]{:S(2)}) async-start(), calls=%async_computation | async-start | bytes 10616832 | tf_op jit(solution)/shard_map/psum | solution.py:205
  8.0 650.9 %collective-permute-start = (s32[3]{0:T(128)S(1)}, s32[3]{0:T(128)S(1)}, u32[]{:S(2)}, u32[]{:S(2)}) collective-permute-start(s32[3]{0:T(128)S(1)} %get-tuple-element.12), channel_id=1, source_target_pairs={{0,8},{8,16},{16,24},{24,32},{32,40},{40,48},{48,56},{56,64},{64,7... | collective-permute-start | bytes 44 | tf_op jit(solution)/shard_map/ppermute | solution.py:12
  10.4 656.3 %collective-permute-start.2 = (s32[3]{0:T(128)S(1)}, s32[3]{0:T(128)S(1)}, u32[]{:S(2)}, u32[]{:S(2)}) collective-permute-start(s32[3]{0:T(128)S(1)} %get-tuple-element.14), channel_id=1, source_target_pairs={{0,1},{1,2},{2,3},{3,4},{4,5},{5,6},{6,7},{8,9},{9,10},{10,11},{11... | collective-permute-start | bytes 44 | tf_op jit(solution)/shard_map/ppermute | solution.py:12
  13.5 647.8 %collective-permute-start.4 = (s32[3]{0:T(128)S(1)}, s32[3]{0:T(128)S(1)}, u32[]{:S(2)}, u32[]{:S(2)}) collective-permute-start(s32[3]{0:T(128)S(1)} %get-tuple-element.17), channel_id=1, source_target_pairs={{0,8},{8,16},{16,24},{24,32},{32,40},{40,48},{48,56},{56,64},{64,7... | collective-permute-start | bytes 44 | tf_op jit(solution)/shard_map/ppermute | solution.py:12
  20.4 601.9 %copy-start.21 = (s32[1,1,3,3]{3,1,2,0:T(1,128)S(1)}, s32[1,1,3,3]{3,1,2,0:T(1,128)}, u32[]{:S(2)}) copy-start(s32[1,1,3,3]{3,1,2,0:T(1,128)} %param.19) | copy-start | bytes 112
  20.4 602.0 %copy-start.18 = (s32[8,16]{1,0:T(8,128)S(1)}, s32[8,16]{1,0:T(8,128)}, u32[]{:S(2)}) copy-start(s32[8,16]{1,0:T(8,128)} %constant.35.clone) | copy-start | bytes 1540
  20.4 602.7 %copy-start.17 = (s32[8,4]{1,0:T(8,128)S(1)}, s32[8,4]{1,0:T(8,128)}, u32[]{:S(2)}) copy-start(s32[8,4]{1,0:T(8,128)} %constant.36.clone) | copy-start | bytes 388
  20.4 603.4 %copy-start.26 = (s32[1,1,12]{2,1,0:T(1,128)S(1)}, s32[1,1,12]{2,1,0:T(1,128)}, u32[]{:S(2)}) copy-start(s32[1,1,12]{2,1,0:T(1,128)} %param.17) | copy-start | bytes 148
  20.4 603.4 %copy-start.16 = (s32[8,16]{1,0:T(8,128)S(1)}, s32[8,16]{1,0:T(8,128)}, u32[]{:S(2)}) copy-start(s32[8,16]{1,0:T(8,128)} %constant.34.clone) | copy-start | bytes 1540
  20.4 604.2 %copy-start.22 = (s32[1,1,2,12]{3,2,1,0:T(2,128)S(1)}, s32[1,1,2,12]{3,2,1,0:T(2,128)}, u32[]{:S(2)}) copy-start(s32[1,1,2,12]{3,2,1,0:T(2,128)} %param.16) | copy-start | bytes 292
  20.4 604.2 %copy-start.15 = (s32[8,64]{1,0:T(8,128)S(1)}, s32[8,64]{1,0:T(8,128)}, u32[]{:S(2)}) copy-start(s32[8,64]{1,0:T(8,128)} %constant.37.clone) | copy-start | bytes 6148
  622.3 29.8 %copy-start.9 = (bf16[3,5,5,5,192]{4,3,2,1,0:T(8,128)(2,1)S(1)}, bf16[3,5,5,5,192]{4,3,2,1,0:T(8,128)(2,1)}, u32[]{:S(2)}) copy-start(bf16[3,5,5,5,192]{4,3,2,1,0:T(8,128)(2,1)} %slice.174) | copy-start | bytes 432004
  622.3 30.5 %copy-start.8 = (bf16[3,5,5,5,192]{4,3,2,1,0:T(8,128)(2,1)S(1)}, bf16[3,5,5,5,192]{4,3,2,1,0:T(8,128)(2,1)}, u32[]{:S(2)}) copy-start(bf16[3,5,5,5,192]{4,3,2,1,0:T(8,128)(2,1)} %slice.175) | copy-start | bytes 432004
  622.3 31.3 %copy-start.7 = (bf16[3,5,5,5,192]{4,3,2,1,0:T(8,128)(2,1)S(1)}, bf16[3,5,5,5,192]{4,3,2,1,0:T(8,128)(2,1)}, u32[]{:S(2)}) copy-start(bf16[3,5,5,5,192]{4,3,2,1,0:T(8,128)(2,1)} %slice.176) | copy-start | bytes 432004
  622.3 32.0 %copy-start.6 = (bf16[3,5,5,5,192]{4,3,2,1,0:T(8,128)(2,1)S(1)}, bf16[3,5,5,5,192]{4,3,2,1,0:T(8,128)(2,1)}, u32[]{:S(2)}) copy-start(bf16[3,5,5,5,192]{4,3,2,1,0:T(8,128)(2,1)} %slice.177) | copy-start | bytes 432004
  622.3 32.7 %copy-start.5 = (bf16[3,5,5,5,192]{4,3,2,1,0:T(8,128)(2,1)S(1)}, bf16[3,5,5,5,192]{4,3,2,1,0:T(8,128)(2,1)}, u32[]{:S(2)}) copy-start(bf16[3,5,5,5,192]{4,3,2,1,0:T(8,128)(2,1)} %slice.178) | copy-start | bytes 432004
  622.3 33.5 %copy-start.4 = (bf16[3,5,5,5,192]{4,3,2,1,0:T(8,128)(2,1)S(1)}, bf16[3,5,5,5,192]{4,3,2,1,0:T(8,128)(2,1)}, u32[]{:S(2)}) copy-start(bf16[3,5,5,5,192]{4,3,2,1,0:T(8,128)(2,1)} %slice.179) | copy-start | bytes 432004
  622.3 34.2 %copy-start.3 = (bf16[3,5,5,5,192]{4,3,2,1,0:T(8,128)(2,1)S(1)}, bf16[3,5,5,5,192]{4,3,2,1,0:T(8,128)(2,1)}, u32[]{:S(2)}) copy-start(bf16[3,5,5,5,192]{4,3,2,1,0:T(8,128)(2,1)} %slice.180) | copy-start | bytes 432004
  622.3 35.0 %copy-start.2 = (bf16[3,5,5,5,192]{4,3,2,1,0:T(8,128)(2,1)S(1)}, bf16[3,5,5,5,192]{4,3,2,1,0:T(8,128)(2,1)}, u32[]{:S(2)}) copy-start(bf16[3,5,5,5,192]{4,3,2,1,0:T(8,128)(2,1)} %slice.181) | copy-start | bytes 432004
  624.6 33.5 %copy-start.19 = (s32[12]{0:T(128)}, s32[12]{0:T(128)S(1)}, u32[]{:S(2)}) copy-start(s32[12]{0:T(128)S(1)} %get-tuple-element.21) | copy-start | bytes 148
  625.6 22.7 %copy-start.14 = (bf16[3,5,5,5,192]{4,3,2,1,0:T(8,128)(2,1)S(1)}, bf16[3,5,5,5,192]{4,3,2,1,0:T(8,128)(2,1)}, u32[]{:S(2)}) copy-start(bf16[3,5,5,5,192]{4,3,2,1,0:T(8,128)(2,1)} %slice.169) | copy-start | bytes 432004
  625.6 23.4 %copy-start.13 = (bf16[3,5,5,5,192]{4,3,2,1,0:T(8,128)(2,1)S(1)}, bf16[3,5,5,5,192]{4,3,2,1,0:T(8,128)(2,1)}, u32[]{:S(2)}) copy-start(bf16[3,5,5,5,192]{4,3,2,1,0:T(8,128)(2,1)} %slice.170) | copy-start | bytes 432004
  625.6 24.2 %copy-start.12 = (bf16[3,5,5,5,192]{4,3,2,1,0:T(8,128)(2,1)S(1)}, bf16[3,5,5,5,192]{4,3,2,1,0:T(8,128)(2,1)}, u32[]{:S(2)}) copy-start(bf16[3,5,5,5,192]{4,3,2,1,0:T(8,128)(2,1)} %slice.171) | copy-start | bytes 432004
  625.6 24.9 %copy-start.11 = (bf16[3,5,5,5,192]{4,3,2,1,0:T(8,128)(2,1)S(1)}, bf16[3,5,5,5,192]{4,3,2,1,0:T(8,128)(2,1)}, u32[]{:S(2)}) copy-start(bf16[3,5,5,5,192]{4,3,2,1,0:T(8,128)(2,1)} %slice.172) | copy-start | bytes 432004
  625.6 25.7 %copy-start.10 = (bf16[3,5,5,5,192]{4,3,2,1,0:T(8,128)(2,1)S(1)}, bf16[3,5,5,5,192]{4,3,2,1,0:T(8,128)(2,1)}, u32[]{:S(2)}) copy-start(bf16[3,5,5,5,192]{4,3,2,1,0:T(8,128)(2,1)} %slice.173) | copy-start | bytes 432004
  658.8 35.4 %copy-start.23 = (s32[3]{0:T(128)}, s32[3]{0:T(128)S(1)}, u32[]{:S(2)}) copy-start(s32[3]{0:T(128)S(1)} %collective-permute-done) | copy-start | bytes 40
  659.1 35.1 %collective-permute-start.8 = (bf16[3,16,192]{2,1,0:T(8,128)(2,1)S(1)}, bf16[3,16,192]{2,1,0:T(8,128)(2,1)S(1)}, u32[]{:S(2)}, u32[]{:S(2)}) collective-permute-start(bf16[3,16,192]{2,1,0:T(8,128)(2,1)S(1)} %reshape.429), channel_id=1, source_target_pairs={{8,0},{16,8},{24,16},{32,24},{40,32},{48,40},{56,48},{64,56},{72,6... | collective-permute-start | bytes 55304 | tf_op jit(solution)/shard_map/ppermute | solution.py:12
  661.3 3.8 collective-permute-start.5
  665.1 3.2 copy-start.25
  665.4 4.6 collective-permute-start.10
  666.7 27.5 %copy-start.24 = (s32[3]{0:T(128)}, s32[3]{0:T(128)S(1)}, u32[]{:S(2)}) copy-start(s32[3]{0:T(128)S(1)} %collective-permute-done.2) | copy-start | bytes 40
  667.0 27.3 %collective-permute-start.9 = (bf16[3,16,192]{2,1,0:T(8,128)(2,1)S(1)}, bf16[3,16,192]{2,1,0:T(8,128)(2,1)S(1)}, u32[]{:S(2)}, u32[]{:S(2)}) collective-permute-start(bf16[3,16,192]{2,1,0:T(8,128)(2,1)S(1)} %reshape.431), channel_id=1, source_target_pairs={{1,0},{2,1},{3,2},{4,3},{5,4},{6,5},{7,6},{9,8},{10,9},{11,10},{12... | collective-permute-start | bytes 55304 | tf_op jit(solution)/shard_map/ppermute | solution.py:12
  670.0 24.2 %collective-permute-start.11 = (bf16[3,4,192]{2,1,0:T(4,128)(2,1)S(1)}, bf16[3,4,192]{2,1,0:T(4,128)(2,1)S(1)}, u32[]{:S(2)}, u32[]{:S(2)}) collective-permute-start(bf16[3,4,192]{2,1,0:T(4,128)(2,1)S(1)} %collective-permute-done.10), channel_id=1, source_target_pairs={{8,0},{16,8},{24,16},{32,24},{40,32},{48,40},{56,48},{64,56},{72,6... | collective-permute-start | bytes 13832 | tf_op jit(solution)/shard_map/ppermute | solution.py:12
  694.9 0.7 copy-start.1
  701.7 9.4 copy-start
  701.8 535.0 %all-reduce.11.cloned.1.call-start = ((), (), s32[]{:S(2)}) async-start(), calls=%async_computation.1 | async-start | bytes 10616832 | tf_op jit(solution)/shard_map/psum | solution.py:205
  715.6 27.6 %collective-permute-start.3 = (bf16[3,16,192]{2,1,0:T(8,128)(2,1)S(1)}, bf16[3,16,192]{2,1,0:T(8,128)(2,1)S(1)}, u32[]{:S(2)}, u32[]{:S(2)}) collective-permute-start(bf16[3,16,192]{2,1,0:T(8,128)(2,1)S(1)} %convolution_convert_fusion.3), channel_id=1, source_target_pairs={{0,1},{1,2},{2,3},{3,4},{4,5},{5,6},{6,7},{8,9},{9,10},{10,11},{11... | collective-permute-start | bytes 55304 | tf_op jit(solution)/shard_map/ppermute | solution.py:12
  721.8 9.1 collective-permute-start.6
  728.6 14.8 %collective-permute-start.1 = (bf16[3,16,192]{2,1,0:T(8,128)(2,1)S(1)}, bf16[3,16,192]{2,1,0:T(8,128)(2,1)}, u32[]{:S(2)}, u32[]{:S(2)}) collective-permute-start(bf16[3,16,192]{2,1,0:T(8,128)(2,1)S(1)} %convolution_convert_fusion.4), channel_id=1, source_target_pairs={{0,8},{8,16},{16,24},{24,32},{32,40},{40,48},{48,56},{56,64},{64,7... | collective-permute-start | bytes 55304 | tf_op jit(solution)/shard_map/ppermute | solution.py:12
  730.9 13.4 %collective-permute-start.7 = (f32[3,4,192]{2,1,0:T(4,128)}, f32[3,4,192]{2,1,0:T(4,128)}, u32[]{:S(2)}, u32[]{:S(2)}) collective-permute-start(f32[3,4,192]{2,1,0:T(4,128)} %collective-permute-done.6), channel_id=1, source_target_pairs={{0,1},{1,2},{2,3},{3,4},{4,5},{5,6},{6,7},{8,9},{9,10},{10,11},{11... | collective-permute-start | bytes 27656 | tf_op jit(solution)/shard_map/ppermute | solution.py:12
  1037.6 2.5 copy-start.20
Sparse Core Ops, SparseCore 0:
  701.9 292.4 all-reduce.8
  997.1 239.6 all-reduce.10
